TPU v7x, 128 devices: a whole 4x4x4 slice. The times are simulated.
128 devices in a mesh: ctx: 8 (over y_lo, x), tp: 16 (over z, y_hi, core).
Axes of the slice: x: 4, y: 4 (y_hi: 2, y_lo: 2; y = y_hi * 2 + y_lo), z: 4, core: 2. Of those that a mesh axis runs over, the one named last changes fastest.
Arguments:
- inputs: bfloat16 [6144, 4096], P('ctx', 'tp'), may hold values from -6 to 6
- in_proj: bfloat16 [4096, 3, 4096], P(None, None, 'tp'), may hold values from -0.125 to 0.125
- out_proj: bfloat16 [4096, 4096], P('tp'), may hold values from -0.125 to 0.125
- short_taps: float32 [7, 3, 4096], P(None, None, 'tp'), may hold values from -2.4 to 2.4
- skip_gain: float32 [4096], P('tp'), may hold values from -4 to 4
- long_taps: bfloat16 [128, 256], P(None, 'tp'), may hold values from -1 to 1
- cotangent: bfloat16 [6144, 4096], P('ctx', 'tp'), may hold values from -1.5 to 1.5
Outputs:
- layer_out: bfloat16 [6144, 4096], P('ctx', 'tp')
- grad_inputs: bfloat16 [6144, 4096], P('ctx', 'tp')
- grad_in_proj: float32 [4096, 3, 4096], P('ctx', None, 'tp')
- grad_out_proj: float32 [4096, 4096], P('tp', 'ctx')
- grad_long_taps: float32 [128, 256], P(None, 'tp')
All inputs are finite; a program needn't handle non-finite values.
Results may differ from a plain program's by a relative error of at most 0.014.
Values may be sent and summed in bfloat16 or wider, within the bound.
A program may use at most 128 MiB of HBM per device.

v0:
```python
import jax
import jax.numpy as jnp
from jax import lax
from jax.sharding import PartitionSpec as P

GROUP = 16
LTAPS = 128
STAPS = 7


def shifted(shard, axis, by):
    peers = lax.axis_size(axis)
    pairs = [(i, i + by) for i in range(peers) if 0 <= i + by < peers]
    return lax.ppermute(shard, axis, pairs)


def tap_sum(padded, tap_table, row_count, causal):
    tap_count = tap_table.shape[0]
    running = jnp.zeros((row_count,) + padded.shape[1:], jnp.float32)
    for lag_index in range(tap_count):
        offset = tap_count - 1 - lag_index if causal else lag_index
        running = running + tap_table[lag_index] * padded[offset : offset + row_count].astype(
            jnp.float32
        )
    return running


def make_bands(tap_table):
    tap_count = tap_table.shape[0]
    row_ids = lax.broadcasted_iota(jnp.int32, (tap_count, tap_count, tap_count), 0)
    col_ids = lax.broadcasted_iota(jnp.int32, (tap_count, tap_count, tap_count), 1)
    tap_ids = lax.broadcasted_iota(jnp.int32, (tap_count, tap_count, tap_count), 2)
    lag_ids = row_ids - col_ids
    lower_hot = (lag_ids == tap_ids).astype(jnp.bfloat16)
    upper_hot = (lag_ids + tap_count == tap_ids).astype(jnp.bfloat16)
    lower_band = jnp.einsum(
        "abj,jg->gab", lower_hot, tap_table, preferred_element_type=jnp.float32
    ).astype(jnp.bfloat16)
    upper_band = jnp.einsum(
        "abj,jg->gab", upper_hot, tap_table, preferred_element_type=jnp.float32
    ).astype(jnp.bfloat16)
    return (lower_band, upper_band)


def lag_totals(matrix):
    group_count = matrix.shape[0]
    tap_count = matrix.shape[1]
    flipped = matrix[:, :, ::-1]
    padded = jnp.pad(flipped, ((0, 0), (0, 0), (0, tap_count)))
    flat_rows = padded.reshape(group_count, 2 * tap_count * tap_count)[
        :, : tap_count * (2 * tap_count - 1)
    ]
    return flat_rows.reshape(group_count, tap_count, 2 * tap_count - 1).sum(axis=1)


def local(inputs, in_proj, out_proj, short_taps, skip_gain, long_taps, cotangent):
    token_count = inputs.shape[0]
    model_width = in_proj.shape[0]
    channels_dev = in_proj.shape[2]
    groups_dev = long_taps.shape[1]
    tile_count = token_count // LTAPS
    in_matrix = in_proj.reshape(model_width, 3 * channels_dev)
    inputs_full = lax.all_gather(inputs, "tp", axis=1, tiled=True)
    projected = jnp.dot(inputs_full, in_matrix, preferred_element_type=jnp.float32).astype(
        jnp.bfloat16
    )
    projected = projected.reshape(token_count, 3, channels_dev)
    short_prev = shifted(projected[token_count - STAPS + 1 :], "ctx", 1)
    mixed = tap_sum(jnp.concatenate([short_prev, projected], axis=0), short_taps, token_count, True)
    query, keyed, valued = (mixed[:, 0], mixed[:, 1], mixed[:, 2])
    gated = (keyed * valued).astype(jnp.bfloat16)
    long_prev = shifted(gated[token_count - LTAPS + 1 :], "ctx", 1)
    lower_band, upper_band = make_bands(long_taps)
    gated_tiles = jnp.concatenate(
        [jnp.zeros((1, channels_dev), jnp.bfloat16), long_prev, gated], axis=0
    )
    gated_tiles = gated_tiles.reshape(tile_count + 1, LTAPS, groups_dev, GROUP)
    gated_now = gated_tiles[1:]
    gated_before = gated_tiles[:-1]
    conv_part = jnp.einsum(
        "gab,nbgc->nagc", lower_band, gated_now, preferred_element_type=jnp.float32
    )
    conv_part = conv_part + jnp.einsum(
        "gab,nbgc->nagc", upper_band, gated_before, preferred_element_type=jnp.float32
    )
    wave = conv_part.reshape(token_count, channels_dev) + skip_gain * gated.astype(jnp.float32)
    filtered = (query * wave).astype(jnp.bfloat16)
    out_terms = jnp.dot(filtered, out_proj, preferred_element_type=jnp.float32)
    layer_out = lax.psum_scatter(
        out_terms.astype(jnp.bfloat16), "tp", scatter_dimension=1, tiled=True
    )
    cot_full = lax.all_gather(cotangent, "tp", axis=1, tiled=True)
    grad_filtered = lax.dot_general(
        cot_full, out_proj, (((1,), (1,)), ((), ())), preferred_element_type=jnp.float32
    )
    out_grad_terms = lax.dot_general(
        filtered, cot_full, (((0,), (0,)), ((), ())), preferred_element_type=jnp.float32
    )
    grad_out_proj = lax.psum_scatter(
        out_grad_terms.astype(jnp.bfloat16), "ctx", scatter_dimension=1, tiled=True
    ).astype(jnp.float32)
    grad_wave = (grad_filtered * query).astype(jnp.bfloat16)
    grad_query = grad_filtered * wave
    wave_next = shifted(grad_wave[: LTAPS - 1], "ctx", -1)
    wave_tiles = jnp.concatenate(
        [grad_wave, wave_next, jnp.zeros((1, channels_dev), jnp.bfloat16)], axis=0
    )
    wave_tiles = wave_tiles.reshape(tile_count + 1, LTAPS, groups_dev, GROUP)
    wave_now = wave_tiles[:-1]
    wave_after = wave_tiles[1:]
    back_part = jnp.einsum(
        "gab,nagc->nbgc", lower_band, wave_now, preferred_element_type=jnp.float32
    )
    back_part = back_part + jnp.einsum(
        "gab,nagc->nbgc", upper_band, wave_after, preferred_element_type=jnp.float32
    )
    grad_gated = back_part.reshape(token_count, channels_dev) + skip_gain * grad_wave.astype(
        jnp.float32
    )
    lower_corr = jnp.einsum(
        "nagc,nbgc->gab", wave_now, gated_now, preferred_element_type=jnp.float32
    )
    upper_corr = jnp.einsum(
        "nagc,nbgc->gab", wave_now, gated_before, preferred_element_type=jnp.float32
    )
    lower_sums = lag_totals(lower_corr)
    upper_sums = lag_totals(upper_corr)
    tap_grads = lower_sums[:, LTAPS - 1 :] + jnp.pad(upper_sums[:, : LTAPS - 1], ((0, 0), (1, 0)))
    grad_long_taps = lax.psum(tap_grads.T, "ctx")
    grad_mixed = jnp.stack([grad_query, grad_gated * valued, grad_gated * keyed], axis=1).astype(
        jnp.bfloat16
    )
    mixed_next = shifted(grad_mixed[: STAPS - 1], "ctx", -1)
    grad_projected = tap_sum(
        jnp.concatenate([grad_mixed, mixed_next], axis=0), short_taps, token_count, False
    )
    grad_matrix = grad_projected.astype(jnp.bfloat16).reshape(token_count, 3 * channels_dev)
    input_terms = lax.dot_general(
        grad_matrix, in_matrix, (((1,), (1,)), ((), ())), preferred_element_type=jnp.float32
    )
    grad_inputs = lax.psum_scatter(
        input_terms.astype(jnp.bfloat16), "tp", scatter_dimension=1, tiled=True
    )
    weight_grad = lax.psum_scatter(
        lax.dot_general(
            inputs_full, grad_matrix, (((0,), (0,)), ((), ())), preferred_element_type=jnp.float32
        ).astype(jnp.bfloat16),
        "ctx",
        scatter_dimension=0,
        tiled=True,
    ).astype(jnp.float32)
    grad_in_proj = weight_grad.reshape(weight_grad.shape[0], 3, channels_dev)
    return (layer_out, grad_inputs, grad_in_proj, grad_out_proj, grad_long_taps)


def solution(mesh):
    placed = (
        P("ctx", "tp"),
        P(None, None, "tp"),
        P("tp", None),
        P(None, None, "tp"),
        P("tp"),
        P(None, "tp"),
        P("ctx", "tp"),
    )
    return jax.shard_map(
        local,
        mesh=mesh,
        in_specs=placed,
        out_specs=(
            P("ctx", "tp"),
            P("ctx", "tp"),
            P("ctx", None, "tp"),
            P("tp", "ctx"),
            P(None, "tp"),
        ),
        check_vma=False,
    )
```

profile of v0, /device:TPU:0, one launch (start us, length us, event | category | flops | bytes accessed | tf_op | source)
XLA Modules:
  0.0 505.0 jit_solution(2170695225887025520)
XLA Ops:
  7.2 0.7 all-gather.3.cloned.1.call-update
  8.0 0.7 all-gather.5.cloned.1.call-update
  8.7 8.7 %copy.27 = bf16[4096,3,256]{0,2,1:T(8,128)(2,1)} copy(bf16[4096,3,256]{2,0,1:T(8,128)(2,1)} %param.8) | data formatting | bytes 12582912 | tf_op args[1]
  17.5 2.2 fusion.9
  19.7 60.1 %all-gather.3.cloned.1.call-done = bf16[768,4096]{1,0:T(8,128)(2,1)} async-done(((bf16[768,256]{1,0:T(8,128)(2,1)}), bf16[768,4096]{1,0:T(8,128)(2,1)}) %all-gather.3.cloned.1.call-update) | async-done | bytes 6291472 | tf_op jit(solution)/shard_map/all_gather | solution.py:63
  79.8 9.0 %convolution_convert_fusion.3 = bf16[768,768]{1,0:T(8,128)(2,1)S(1)} fusion(bf16[768,4096]{1,0:T(8,128)(2,1)} %all-gather.3.cloned.1.call-done, bf16[4096,768]{0,1:T(8,128)(2,1)} %bitcast.122), kind=kOutput, calls=%fused_computation.18 | convolution fusion | flops 4832428032 | bytes 13762560 | tf_op jit(solution)/shard_map/dot_general | solution.py:64
  88.8 3.4 collective-permute-start
  92.2 2.5 fusion.8
  94.8 1.4 copy.28
  96.2 1.6 copy.29
  97.8 2.1 multiply_add_fusion
  100.0 1.4 copy-done.1
  101.4 0.8 multiply_convert_fusion.3
  102.2 44.4 %all-gather.5.cloned.1.call-done = bf16[768,4096]{1,0:T(8,128)(2,1)} async-done(((bf16[768,256]{1,0:T(8,128)(2,1)}), bf16[768,4096]{1,0:T(8,128)(2,1)}) %all-gather.5.cloned.1.call-update) | async-done | bytes 6291472 | tf_op jit(solution)/shard_map/all_gather | solution.py:92
  146.6 6.2 %multiply_convert_fusion = (bf16[768,256]{1,0:T(8,128)(2,1)S(1)}, bf16[768,256]{1,0:T(8,128)(2,1)S(1)}, f32[768,256]{1,0:T(8,128)}) fusion(f32[768,3,256]{2,0,1:T(8,128)} %copy-done.1, bf16[768,4096]{1,0:T(8,128)(2,1)} %all-gather.5.cloned.1.call-done, bf16[256,4096]{1,0:T(8,128)(2,1)S(1)} %copy-done), kind=kOutput, calls=%fused_computation.50 | convolution fusion | flops 1611399168 | bytes 12320768 | tf_op jit(solution)/shard_map/dot_general | solution.py:93
  153.4 0.9 copy.40
  154.3 1.9 copy.32
  156.2 2.3 convert_element_type.117
  158.5 0.6 slice.168
  159.1 1.3 collective-permute-start.2
  160.4 4.7 collective-permute-start.1
  165.1 2.2 slice.139
  167.4 2.4 fusion.22
  169.8 1.5 fusion.20
  171.3 1.9 pad_maximum_fusion.3
  173.3 1.2 copy.43
  174.4 1.2 slice.142
  175.7 1.5 fusion.5
  177.6 1.2 copy.47
  178.8 1.9 copy.35
  180.7 1.4 slice.138
  182.2 1.8 fusion.6
  184.4 1.2 copy.39
  185.6 3.0 fusion.26
  188.6 0.7 copy-done.2
  189.3 5.9 %convolution_convert_fusion.2 = bf16[256,4096]{1,0:T(8,128)(2,1)} fusion(bf16[768,256]{1,0:T(8,128)(2,1)S(1)} %get-tuple-element.17, bf16[768,4096]{1,0:T(8,128)(2,1)} %all-gather.5.cloned.1.call-done), kind=kOutput, calls=%fused_computation.9 | convolution fusion | flops 1611661312 | bytes 8781824 | tf_op jit(solution)/shard_map/dot_general | solution.py:96
  195.5 1.3 collective-permute-start.3
  196.8 4.3 collective-permute-done.3
  201.2 3.0 add_convert_fusion
  204.2 1.6 copy.48
  205.7 9.7 %fusion.2 = bf16[4096,768]{0,1:T(8,128)(2,1)} fusion(bf16[768,768]{0,1:T(8,128)(2,1)S(1)} %bitcast.128, bf16[768,4096]{1,0:T(8,128)(2,1)} %all-gather.3.cloned.1.call-done), kind=kOutput, calls=%fused_computation.8 | convolution fusion | flops 4834983936 | bytes 13762560 | tf_op jit(solution)/shard_map/dot_general | solution.py:145
  215.5 0.9 copy-done.3
  216.5 4.4 convolution_convert_fusion
  221.2 1.0 copy-done.4
  222.2 9.7 %bitcast_convert_fusion = bf16[768,4096]{1,0:T(8,128)(2,1)} fusion(bf16[768,3,256]{2,0,1:T(8,128)(2,1)S(1)} %copy-done.4, bf16[4096,3,256]{2,0,1:T(8,128)(2,1)} %param.8), kind=kOutput, calls=%fused_computation | convolution fusion | flops 4834983936 | bytes 13762560 | tf_op jit(solution)/shard_map/dot_general | solution.py:138
  231.9 1.0 copy-done.11
  233.1 1.3 convolution_bitcast_fusion.1
  234.4 7.5 %rev.6 = f32[16,128,128]{2,1,0:T(8,128)S(1)} reverse(f32[16,128,128]{2,1,0:T(8,128)} %convolution_bitcast_fusion.1), dimensions={2} | reverse | bytes 2097152 | tf_op jit(solution)/shard_map/rev | solution.py:48
  242.2 1.2 copy.77
  243.4 1.5 slice.177
  244.9 6.4 %reshape.63 = f32[16,128,255]{2,1,0:T(8,128)} reshape(f32[16,32640]{1,0:T(8,128)} %slice.177) | data formatting | bytes 4177920 | tf_op jit(solution)/shard_map/reshape | solution.py:53
  251.3 1.8 reduce_sum.18
  253.1 1.3 convolution_bitcast_fusion
  254.4 7.5 %rev.7 = f32[16,128,128]{2,1,0:T(8,128)S(1)} reverse(f32[16,128,128]{2,1,0:T(8,128)} %convolution_bitcast_fusion), dimensions={2} | reverse | bytes 2097152 | tf_op jit(solution)/shard_map/rev | solution.py:48
  262.1 1.2 copy.78
  263.4 1.5 slice.179
  264.9 6.2 %reshape.65 = f32[16,128,255]{2,1,0:T(8,128)} reshape(f32[16,32640]{1,0:T(8,128)} %slice.179) | data formatting | bytes 4177920 | tf_op jit(solution)/shard_map/reshape | solution.py:53
  271.1 1.8 reduce_sum.19
  272.9 22.4 %psum.7 = f32[128,16]{0,1:T(8,128)} all-reduce(f32[128,16]{0,1:T(8,128)S(1)} %fusion.35), channel_id=1, replica_groups=mesh['ctx'=8,'tp'=16] {'ctx'}, use_global_device_ids=true, to_apply=%region_6.7 | all-reduce | flops 2048 | bytes 16384 | tf_op jit(solution)/shard_map/psum | solution.py:129
  295.3 1.8 convert_element_type.140
  297.1 14.2 %reduce-scatter.9.cloned.1.call-done = bf16[512,768]{0,1:T(8,128)(2,1)} async-done(((bf16[4096,768]{0,1:T(8,128)(2,1)}), bf16[512,768]{0,1:T(8,128)(2,1)}) %reduce-scatter.9.cloned.1.call-update) | async-done | bytes 786448 | tf_op jit(solution)/shard_map/reduce_scatter | solution.py:144
  311.3 2.5 copy.53
  313.9 90.6 %reduce-scatter.5.cloned.1.call-done = bf16[768,256]{1,0:T(8,128)(2,1)} async-done(((bf16[768,4096]{1,0:T(8,128)(2,1)}), bf16[768,256]{1,0:T(8,128)(2,1)}) %reduce-scatter.5.cloned.1.call-update) | async-done | bytes 393232 | tf_op jit(solution)/shard_map/reduce_scatter | solution.py:89
  404.5 93.7 %reduce-scatter.7.cloned.1.call-done = bf16[768,256]{1,0:T(8,128)(2,1)} async-done(((bf16[768,4096]{1,0:T(8,128)(2,1)}), bf16[768,256]{1,0:T(8,128)(2,1)}) %reduce-scatter.7.cloned.1.call-update) | async-done | bytes 393232 | tf_op jit(solution)/shard_map/reduce_scatter | solution.py:141
  (74 shorter events, 3.0 us)
Async XLA Ops:
  7.2 139.4 %copy-start = (bf16[256,4096]{1,0:T(8,128)(2,1)S(1)}, bf16[256,4096]{1,0:T(8,128)(2,1)}, u32[]{:S(2)}) copy-start(bf16[256,4096]{1,0:T(8,128)(2,1)} %param.9) | copy-start | bytes 6291460
  7.2 72.6 %all-gather.3.cloned.1.call-start = ((), (), s32[]{:S(2)}) async-start(), calls=%async_computation.4 | async-start | bytes 6684672 | tf_op jit(solution)/shard_map/all_gather | solution.py:63
  7.9 138.7 %all-gather.5.cloned.1.call-start = ((), (), s32[]{:S(2)}) async-start(), calls=%async_computation.6 | async-start | bytes 6684672 | tf_op jit(solution)/shard_map/all_gather | solution.py:92
  8.7 8.8 %copy-start.20 = (f32[7,3,256]{2,0,1:T(8,128)S(1)}, f32[7,3,256]{2,0,1:T(8,128)}, u32[]{:S(2)}) copy-start(f32[7,3,256]{2,0,1:T(8,128)} %param.10) | copy-start | bytes 64516
  8.7 8.8 %copy-start.22 = (bf16[128,16]{0,1:T(8,128)(2,1)S(1)}, bf16[128,16]{0,1:T(8,128)(2,1)}, u32[]{:S(2)}) copy-start(bf16[128,16]{0,1:T(8,128)(2,1)} %param.12) | copy-start | bytes 12292
  8.7 286.6 %reduce-scatter.11.cloned.1.call-start = ((), (), s32[]{:S(2)}) async-start(), calls=%async_computation.9 | async-start | bytes 2359296 | tf_op jit(solution)/shard_map/reduce_scatter | solution.py:99
  17.5 80.3 %copy-start.14 = (f32[3,256]{1,0:T(4,128)}, f32[3,256]{1,0:T(4,128)S(1)}, u32[]{:S(2)}) copy-start(f32[3,256]{1,0:T(4,128)S(1)} %get-tuple-element.31) | copy-start | bytes 9220
  17.5 80.3 %copy-start.16 = (f32[3,256]{1,0:T(4,128)}, f32[3,256]{1,0:T(4,128)S(1)}, u32[]{:S(2)}) copy-start(f32[3,256]{1,0:T(4,128)S(1)} %get-tuple-element.32) | copy-start | bytes 9220
  88.8 8.9 %collective-permute-start = (bf16[6,3,256]{2,0,1:T(8,128)(2,1)S(1)}, bf16[6,3,256]{2,0,1:T(8,128)(2,1)S(1)}, u32[]{:S(2)}, u32[]{:S(2)}) collective-permute-start(bf16[6,3,256]{2,0,1:T(8,128)(2,1)S(1)} %bitcast.132), channel_id=1, source_target_pairs={{0,16},{16,32},{32,48},{48,64},{64,80},{80,96},{96,112},{1,17},{17... | collective-permute-start | bytes 27656 | tf_op jit(solution)/shard_map/ppermute | solution.py:14
  94.8 3.0 copy-start.18
  100.0 1.4 copy-start.1
  152.8 14.6 %copy-start.8 = (bf16[768,256]{1,0:T(8,128)(2,1)}, bf16[768,256]{1,0:T(8,128)(2,1)S(1)}, u32[]{:S(2)}) copy-start(bf16[768,256]{1,0:T(8,128)(2,1)S(1)} %get-tuple-element.19) | copy-start | bytes 1179652
  152.8 18.6 %copy-start.5 = (bf16[768,256]{1,0:T(8,128)(2,1)}, bf16[768,256]{1,0:T(8,128)(2,1)S(1)}, u32[]{:S(2)}) copy-start(bf16[768,256]{1,0:T(8,128)(2,1)S(1)} %get-tuple-element.18) | copy-start | bytes 1179652
  152.8 14.6 %copy-start.7 = (bf16[16,128,128,1]{2,0,1,3:T(8,128)(2,1)S(1)}, bf16[16,128,128,1]{2,0,1,3:T(8,128)(2,1)}, u32[]{:S(2)}) copy-start(bf16[16,128,128,1]{2,0,1,3:T(8,128)(2,1)} %fusion.8) | copy-start | bytes 1572868
  159.1 12.2 %collective-permute-start.2 = (bf16[127,256]{1,0:T(8,128)(2,1)}, bf16[127,256]{1,0:T(8,128)(2,1)S(1)}, u32[]{:S(2)}, u32[]{:S(2)}) collective-permute-start(bf16[127,256]{1,0:T(8,128)(2,1)} %slice.169), channel_id=1, source_target_pairs={{16,0},{32,16},{48,32},{64,48},{80,64},{96,80},{112,96},{17,1},{33... | collective-permute-start | bytes 195080 | tf_op jit(solution)/shard_map/ppermute | solution.py:14
  160.4 10.9 %collective-permute-start.1 = (bf16[127,256]{1,0:T(8,128)(2,1)}, bf16[127,256]{1,0:T(8,128)(2,1)S(1)}, u32[]{:S(2)}, u32[]{:S(2)}) collective-permute-start(bf16[127,256]{1,0:T(8,128)(2,1)} %slice.168), channel_id=1, source_target_pairs={{0,16},{16,32},{32,48},{48,64},{64,80},{80,96},{96,112},{1,17},{17... | collective-permute-start | bytes 195080 | tf_op jit(solution)/shard_map/ppermute | solution.py:14
  177.4 4.7 copy-start.6
  182.1 2.1 copy-start.9
  184.0 1.6 copy-start.21
  188.5 0.7 copy-start.2
  195.2 116.1 %reduce-scatter.9.cloned.1.call-start = ((), (), s32[]{:S(2)}) async-start(), calls=%async_computation.8 | async-start | bytes 7077888 | tf_op jit(solution)/shard_map/reduce_scatter | solution.py:144
  195.3 5.9 %copy-start.15 = (f32[3,256]{1,0:T(4,128)S(1)}, f32[3,256]{1,0:T(4,128)}, u32[]{:S(2)}) copy-start(f32[3,256]{1,0:T(4,128)} %copy-done.14) | copy-start | bytes 9220
  195.3 5.9 %copy-start.17 = (f32[3,256]{1,0:T(4,128)S(1)}, f32[3,256]{1,0:T(4,128)}, u32[]{:S(2)}) copy-start(f32[3,256]{1,0:T(4,128)} %copy-done.16) | copy-start | bytes 9220
  195.3 5.9 %copy-start.19 = (f32[1,3,256]{2,1,0:T(4,128)S(1)}, f32[1,3,256]{2,1,0:T(4,128)}, u32[]{:S(2)}) copy-start(f32[1,3,256]{2,1,0:T(4,128)} %copy-done.18) | copy-start | bytes 9220
  195.5 5.6 %collective-permute-start.3 = (bf16[6,3,256]{2,0,1:T(8,128)(2,1)S(1)}, bf16[6,3,256]{2,0,1:T(8,128)(2,1)S(1)}, u32[]{:S(2)}, u32[]{:S(2)}) collective-permute-start(bf16[6,3,256]{2,0,1:T(8,128)(2,1)S(1)} %slice.170), channel_id=1, source_target_pairs={{16,0},{32,16},{48,32},{64,48},{80,64},{96,80},{112,96},{17,1},{33... | collective-permute-start | bytes 27656 | tf_op jit(solution)/shard_map/ppermute | solution.py:14
  215.5 1.0 copy-start.3
  215.5 189.0 %reduce-scatter.5.cloned.1.call-start = ((), (), s32[]{:S(2)}) async-start(), calls=%async_computation.5 | async-start | bytes 6684672 | tf_op jit(solution)/shard_map/reduce_scatter | solution.py:89
  220.9 1.3 copy-start.4
  220.9 277.3 %reduce-scatter.7.cloned.1.call-start = ((), (), s32[]{:S(2)}) async-start(), calls=%async_computation.7 | async-start | bytes 6684672 | tf_op jit(solution)/shard_map/reduce_scatter | solution.py:141
  231.9 1.0 copy-start.11
  231.9 1.2 copy-start.13
  244.9 8.1 %copy-start.10 = (bf16[6,128,16,16]{1,0,3,2:T(8,128)(2,1)S(1)}, bf16[6,128,16,16]{1,0,3,2:T(8,128)(2,1)}, u32[]{:S(2)}) copy-start(bf16[6,128,16,16]{1,0,3,2:T(8,128)(2,1)} %copy-done.9) | copy-start | bytes 1179652
  244.9 8.1 %copy-start.12 = (bf16[6,128,16,16]{1,0,3,2:T(8,128)(2,1)S(1)}, bf16[6,128,16,16]{1,0,3,2:T(8,128)(2,1)}, u32[]{:S(2)}) copy-start(bf16[6,128,16,16]{1,0,3,2:T(8,128)(2,1)} %slice.139) | copy-start | bytes 1179652
Sparse Core Ops, SparseCore 0:
  10.4 69.3 all-gather.2
  82.1 64.4 all-gather.4
  195.4 41.2 reduce-scatter.10
  239.0 72.3 reduce-scatter.8
  316.0 88.4 reduce-scatter.4
  409.7 88.4 reduce-scatter.6
where the time goes:
time: 507 us; the launch traced here: 505 us
  waiting for transfers between devices  309 us (61%)
  local copies, waits for them, and re-layouts  72.2 us (14%)
  matrix products  59.6 us (12%)
  blocking collectives  22.4 us (4%)
  other arithmetic  16.4 us (3%)
  between operations  14.6 us (3%)
  starting transfers between devices  11.1 us (2%)
    reduce_scatter x1, waiting for transfers between devices, local(): lax.psum_scatter(input_terms.astype(jnp.bfloat16), 'tp', scatter_dimensio...  93.7 us
    reduce_scatter x1, waiting for transfers between devices, local(): lax.psum_scatter(out_terms.astype(jnp.bfloat16), 'tp', scatter_dimension=...  90.6 us
    all_gather x1, waiting for transfers between devices, local(): inputs_full = lax.all_gather(inputs, 'tp', axis=1, tiled=True)  60.1 us
    all_gather x1, waiting for transfers between devices, local(): cot_full = lax.all_gather(cotangent, 'tp', axis=1, tiled=True)  44.4 us
    psum x1, blocking collectives, local(): grad_long_taps = lax.psum(tap_grads.T, 'ctx')  22.4 us
    unnamed x56, local copies, waits for them, and re-layouts  19.3 us
    rev x2, local copies, waits for them, and re-layouts, lag_totals(): flipped = matrix[:, :, ::-1]  15 us
    reduce_scatter x1, waiting for transfers between devices, local(): lax.psum_scatter(lax.dot_general(inputs_full, grad_matrix, (((0,), (0,)),...  14.2 us
  transfers between devices with their start and end apart: 10, of which 6 were waited for; matrix products, arithmetic and copies ran while one was open for 21% of the time, Pallas kernels for 0%

commit v1 on v0

v1 whole, which is shorter than its diff:
```python
import jax
import jax.numpy as jnp
from jax import lax
from jax.experimental import pallas as pl
from jax.experimental.pallas import tpu as pltpu
from jax.sharding import PartitionSpec as P

GROUP = 16
LTAPS = 128
STAPS = 7
MESH = pl.DeviceIdType.MESH
F32 = jnp.float32
BF16 = jnp.bfloat16
T = 768
C = 256
NT = T // LTAPS
HALF = T // 2


def dot(a, b, dims=((1,), (0,))):
    return lax.dot_general(a, b, (dims, ((), ())), preferred_element_type=F32)


def remote(src, dst, send, recv, where):
    return pltpu.make_async_remote_copy(
        src_ref=src, dst_ref=dst, send_sem=send, recv_sem=recv, device_id=where, device_id_type=MESH
    )


class Gather:
    def __init__(self, src, buf, send, recv, z, h, k):
        self.src, self.buf = src, buf
        zp, zm, zo = lax.rem(z + 1, 4), lax.rem(z + 3, 4), lax.rem(z + 2, 4)

        def at(zz, hh, kk):
            return zz * 4 + hh * 2 + kk

        g, q = 1 - h, 1 - k
        plus, minus = {"tp": at(zp, h, k)}, {"tp": at(zm, h, k)}
        side, mate = {"tp": at(z, g, k)}, {"tp": at(z, h, q)}
        own = at(z, h, k)
        first, second = pl.ds(0, HALF), pl.ds(HALF, HALF)
        whole = pl.ds(0, T)
        plan = [
            (own, whole, plus),
            (own, whole, minus),
            (own, whole, side),
            (own, whole, mate),
            (at(z, g, k), whole, plus),
            (at(z, g, k), whole, minus),
            (at(z, g, k), whole, mate),
            (at(zm, h, k), first, plus),
            (at(zp, h, k), second, minus),
            (at(zm, h, k), whole, mate),
            (at(zp, h, k), whole, mate),
            (at(zm, g, k), first, plus),
            (at(zp, g, k), second, minus),
            (at(zm, g, k), whole, mate),
            (at(zp, g, k), whole, mate),
            (at(zo, h, k), whole, mate),
            (at(zo, g, k), whole, mate),
        ]
        self.copies = []
        for i, (slot, rows, where) in enumerate(plan):
            source = src if i < 4 else buf.at[slot, rows]
            self.copies.append(remote(source, buf.at[slot, rows], send.at[i], recv.at[i], where))
        self.groups = [
            (own, at(z, h, q)),
            (at(zm, h, k), at(zp, h, k)),
            (at(zm, h, q), at(zp, h, q)),
            (at(z, g, k), at(z, g, q)),
            (at(zm, g, k), at(zp, g, k)),
            (at(zm, g, q), at(zp, g, q)),
            (at(zo, h, k), at(zo, h, q)),
            (at(zo, g, k), at(zo, g, q)),
        ]

    def start(self, *which):
        for i in which:
            self.copies[i].start()

    def wait(self, *which):
        for i in which:
            self.copies[i].wait_recv()

    def drain(self):
        for copy in self.copies:
            copy.wait_send()


class Ring:
    def __init__(self, out, inn, side_out, side_in, send, recv, plus, minus, side, part):
        self.out, self.inn, self.side_out, self.side_in = out, inn, side_out, side_in
        self.part = part
        self.copies = []
        for kind in range(2):
            for i, (low, size, where) in enumerate([(0, 1, plus), (1, 1, minus), (2, 2, plus), (4, 2, minus)]):
                span = pl.ds(low, size)
                self.copies.append(
                    remote(out.at[kind, span], inn.at[kind, span], send.at[kind * 4 + i], recv.at[kind * 4 + i], where)
                )
        self.copies.append(remote(side_out, side_in, send.at[8], recv.at[8], side))

    def first(self, kind):
        for half in range(2):
            self.part("o", kind, half, [], self.out.at[kind, half])
            self.copies[kind * 4 + half].start()

    def second(self, kind):
        o, r = self.out, self.inn
        self.copies[kind * 4].wait_recv()
        self.part("p", kind, 0, [r.at[kind, 0]], o.at[kind, 2])
        self.part("p", kind, 1, [], o.at[kind, 3])
        self.copies[kind * 4 + 2].start()
        self.copies[kind * 4 + 1].wait_recv()
        self.part("m", kind, 0, [], o.at[kind, 4])
        self.part("m", kind, 1, [r.at[kind, 1]], o.at[kind, 5])
        self.copies[kind * 4 + 3].start()

    def third(self):
        r = self.inn
        self.copies[6].wait_recv()
        self.copies[7].wait_recv()
        for half in range(2):
            self.part("c", 1, half, [r.at[1, 2 + half], r.at[1, 4 + half]], self.side_out.at[half])
        self.copies[8].start()

    def last(self, targets):
        r = self.inn
        self.copies[2].wait_recv()
        self.copies[3].wait_recv()
        self.copies[8].wait_recv()
        for half in range(2):
            self.part("c", 0, half, [r.at[0, 2 + half], r.at[0, 4 + half], self.side_in.at[half]], targets[half])

    def drain(self):
        for copy in self.copies:
            copy.wait_send()


def body(
    inputs_ref, cot_ref, w_hbm, op_hbm, staps_ref, skip_ref, hrev_ref, hfwd_ref,
    lo_out, gi_out, gin_out, gout_out, taps_out,
    X, Y, W, OP, PF, QKV, WAVE, GF, FIL, FT, GM, GT, GWT, TT, HS, HR, HT, TG, TGR, GOS, LOS, GIS,
    SP, LRP, GRP, S, LR, GR, SY, LRY, GRY, CS, CR, CSY, CRY, OS, OR, OSY, ORY,
    xs, xr, ys, yr, lps, lpr, gps, gpr, ls, lr, gs, gr, cs, cr, os_, or_, hs, hr, ts, tr, loc,
):
    ctx = lax.axis_index("ctx")
    me = lax.axis_index("tp")
    z, h, k = me // 4, lax.rem(me // 2, 2), lax.rem(me, 2)
    l, x = ctx // 4, lax.rem(ctx, 4)

    def at(zz, hh, kk):
        return zz * 4 + hh * 2 + kk

    zp, zm, zo = lax.rem(z + 1, 4), lax.rem(z + 3, 4), lax.rem(z + 2, 4)
    xp, xm, xo = lax.rem(x + 1, 4), lax.rem(x + 3, 4), lax.rem(x + 2, 4)
    mate = {"tp": at(z, h, 1 - k)}

    barrier = pltpu.get_barrier_semaphore()
    peers = [{"tp": at(zp, h, k)}, {"tp": at(zm, h, k)}, {"tp": at(z, 1 - h, k)}, mate]
    peers += [{"ctx": lax.rem(ctx + i, 8)} for i in range(1, 8)]
    for peer in peers:
        pl.semaphore_signal(barrier, inc=1, device_id=peer, device_id_type=MESH)
    pl.semaphore_wait(barrier, len(peers))

    gx = Gather(inputs_ref, X, xs, xr, z, h, k)
    gy = Gather(cot_ref, Y, ys, yr, z, h, k)
    gx.start(2, 0, 1, 3)
    loads = [
        pltpu.make_async_copy(inputs_ref, X.at[me], loc.at[0]),
        pltpu.make_async_copy(w_hbm, W, loc.at[1]),
        pltpu.make_async_copy(op_hbm, OP, loc.at[2]),
        pltpu.make_async_copy(cot_ref, Y.at[me], loc.at[3]),
    ]
    for load in loads:
        load.start()

    def project(index, fresh=False):
        a, b = gx.groups[index]

        def one(s, _):
            for at_half in range(2):
                rows = pl.ds(at_half * HALF, HALF)
                to = pl.ds(8 + at_half * HALF, HALF)
                total = dot(X[a, rows], W[s, pl.ds(pl.multiple_of(a * C, C), C), :])
                total = total + dot(X[b, rows], W[s, pl.ds(pl.multiple_of(b * C, C), C), :])
                PF[s, to, :] = total if fresh else PF[s, to, :] + total
            return 0

        lax.fori_loop(0, 3, one, 0)

    loads[0].wait()
    loads[1].wait()
    gx.wait(3)
    project(0, True)
    gx.wait(0)
    gx.start(7, 9)
    gx.wait(1)
    gx.start(8, 10)
    project(1)
    gx.wait(2)
    gx.start(4, 5, 6)
    gy.start(2)
    gx.wait(9, 10)
    project(2)
    gx.wait(6)
    project(3)
    gx.wait(7, 8)
    gx.start(15)
    gx.wait(4)
    gx.start(11, 13)
    gx.wait(5)
    gx.start(12, 14)
    gy.start(0, 1, 3)
    project(4)
    gx.wait(15)
    project(6)
    gx.wait(13, 14)
    project(5)
    gx.wait(11, 12)
    gx.start(16)
    gx.wait(16)
    project(7)

    def round_rows(i, _):
        s, r = i // NT, lax.rem(i, NT)
        rows = pl.ds(pl.multiple_of(8 + r * LTAPS, 8), LTAPS)
        PF[s, rows, :] = PF[s, rows, :].astype(BF16).astype(F32)
        return 0

    nxt, prv = {"ctx": lax.rem(ctx + 1, 8)}, {"ctx": lax.rem(ctx + 7, 8)}
    for s in range(3):
        HS[0, s] = PF[s, T - 8 : T + 8, :].astype(BF16)
    halo0 = remote(HS.at[0], HR.at[0], hs.at[0], hr.at[0], nxt)
    halo0.start()
    lax.fori_loop(0, 3 * NT, round_rows, 0)
    gy.wait(2)
    gy.start(4, 5, 6)
    gy.wait(0)
    gy.start(7, 9)
    gy.wait(1)
    gy.start(8, 10)
    halo0.wait_recv()
    begins, ends = ctx == 0, ctx == 7
    for s in range(3):
        tail = HR[0, s].astype(F32)[8:16]
        PF[s, 0:8, :] = jnp.where(begins, 0.0, tail)

    def short_forward(i, _):
        s, r = i // NT, lax.rem(i, NT)
        window = PF[s, pl.ds(pl.multiple_of(r * LTAPS, 8), LTAPS + 8), :]
        total = staps_ref[s, 0:1, :] * window[8:]
        for j in range(1, STAPS):
            total = total + staps_ref[s, j : j + 1, :] * pltpu.roll(window, j, 0)[8:]
        QKV[s, pl.ds(pl.multiple_of(r * LTAPS, LTAPS), LTAPS), :] = total
        return 0

    lax.fori_loop(0, 3 * NT, short_forward, 0)

    def tile_rows(n):
        return pl.ds(pl.multiple_of(n * LTAPS, LTAPS), LTAPS)

    def gated_tile(n):
        return (QKV[1, tile_rows(n), :] * QKV[2, tile_rows(n), :]).astype(BF16).astype(F32)

    def put_gated(n, _):
        GT[n + 1] = gated_tile(n).T.astype(BF16)
        return 0

    lax.fori_loop(0, NT, put_gated, 0)
    halo1 = remote(GT.at[NT], HT.at[0], hs.at[1], hr.at[1], nxt)
    halo1.start()
    gy.wait(4)
    gy.start(11, 13)
    gy.wait(5)
    gy.start(12, 14)
    gy.wait(7, 8)
    gy.start(15)
    halo1.wait_recv()
    GT[0] = jnp.where(begins, 0.0, HT[0].astype(F32)).astype(BF16)

    def windows(ref, rows):
        return jnp.concatenate(
            [jnp.concatenate([ref[n, rows, :], ref[n + 1, rows, :]], axis=1) for n in range(NT)], axis=0
        )

    def band_of(ref, g):
        spread = jnp.broadcast_to(ref[g], (LTAPS, 2 * LTAPS))
        return pltpu.roll(spread, 0, 1, stride=1, stride_axis=0).astype(BF16)

    def convolve(g, _):
        rows = pl.ds(pl.multiple_of(g * GROUP, GROUP), GROUP)
        got = dot(windows(GT, rows), band_of(hrev_ref, g), ((1,), (1,)))
        for n in range(NT):
            TT[n, rows, :] = got[n * GROUP : (n + 1) * GROUP]
        return 0

    lax.fori_loop(0, GROUP, convolve, 0)

    for n in range(NT):
        rows = pl.ds(n * LTAPS, LTAPS)
        wave = TT[n].T + skip_ref[...] * gated_tile(n)
        WAVE[rows, :] = wave
        fil = (QKV[0, rows, :] * wave).astype(BF16)
        FIL[rows, :] = fil
        FT[:, rows] = fil.astype(F32).T.astype(BF16)

    def lo_part(slot, half):
        return dot(FIL[pl.ds(half * HALF, HALF), :], OP[:, pl.ds(pl.multiple_of(slot * C, C), C)])

    def gi_part(slot, half):
        rows = pl.ds(half * HALF, HALF)
        picked = pl.ds(pl.multiple_of(slot * C, C), C)
        total = dot(GM[0, rows, :], W[0, picked, :], ((1,), (1,)))
        total = total + dot(GM[1, rows, :], W[1, picked, :], ((1,), (1,)))
        return total + dot(GM[2, rows, :], W[2, picked, :], ((1,), (1,)))

    def for_mate(part, pairs):
        for index, pair in enumerate(pairs):
            def one(half, _, index=index):
                i = index
                zz, hh = (zo, zp, zm, z)[i // 2], (1 - h, h)[i % 2]
                SP[i, half] = part(at(zz, hh, 1 - k), half).astype(BF16)
                return 0

            lax.fori_loop(0, 2, one, 0)
            pair.start()

    def mate_pairs(into, send, recv):
        return [remote(SP.at[i], into.at[i], send.at[i], recv.at[i], mate) for i in range(8)]

    def tp_ring(part, from_mate, pairs, inn, side_in, send, recv):
        def term(name, kind, half, extra, target):
            place = {"o": 0, "p": 1, "m": 2, "c": 3}[name]
            index = place * 2 + (0 if kind == 1 else 1)
            if half == 0:
                pairs[index].wait_recv()
            zz = (zo, zp, zm, z)[place]
            hh = 1 - h if kind == 1 else h
            total = part(at(zz, hh, k), half) + from_mate[index, half].astype(F32)
            for ref in extra:
                total = total + ref[...].astype(F32)
            target[...] = total.astype(target.dtype)

        return Ring(
            S, inn, SY, side_in, send, recv,
            {"tp": at(zp, h, k)}, {"tp": at(zm, h, k)}, {"tp": at(z, 1 - h, k)}, term,
        )

    def ctx_ring(fill, out, inn, side_out, side_in, send, recv):
        def term(name, kind, half, extra, target):
            xx = {"o": xo, "p": xp, "m": xm, "c": x}[name]
            ll = 1 - l if kind == 1 else l
            fill((ll * 4 + xx) * 2 + half, half, extra, target)

        return Ring(
            out, inn, side_out, side_in, send, recv,
            {"ctx": l * 4 + xp}, {"ctx": l * 4 + xm}, {"ctx": (1 - l) * 4 + x}, term,
        )

    loads[2].wait()
    lo_pairs = mate_pairs(LRP, lps, lpr)
    for_mate(lo_part, lo_pairs)

    def filter_grad(index, fresh=False):
        a, b = gy.groups[index]

        def one(i, _):
            rows = pl.ds(pl.multiple_of(i * HALF, HALF), HALF)
            total = dot(Y[a, rows, :], OP[:, pl.ds(pl.multiple_of(a * C, C), C)], ((1,), (1,)))
            total = total + dot(Y[b, rows, :], OP[:, pl.ds(pl.multiple_of(b * C, C), C)], ((1,), (1,)))
            GF[rows, :] = total if fresh else GF[rows, :] + total
            return 0

        lax.fori_loop(0, 2, one, 0)

    loads[3].wait()
    gy.wait(3)
    filter_grad(0, True)
    filter_grad(1)
    gy.wait(9, 10)
    filter_grad(2)
    gy.wait(6)
    filter_grad(3)
    gy.wait(11, 12)
    gy.start(16)
    filter_grad(4)
    gy.wait(15)
    filter_grad(6)
    gy.wait(13, 14)
    filter_grad(5)
    gy.wait(16)
    filter_grad(7)

    def put_grad_wave(n, _):
        rows = tile_rows(n)
        GWT[n] = (GF[rows, :] * QKV[0, rows, :]).astype(BF16).astype(F32).T.astype(BF16)
        return 0

    lax.fori_loop(0, NT, put_grad_wave, 0)
    halo2 = remote(GWT.at[0], HT.at[1], hs.at[2], hr.at[2], prv)
    halo2.start()

    def go_fill(slot, half, extra, target):
        total = dot(FT[...], Y[slot])
        for ref in extra:
            total = total + ref[0].astype(F32)
        target[0] = total.astype(target.dtype)

    go = ctx_ring(go_fill, OS, OR, OSY, ORY, os_, or_)
    go.first(1)
    go.first(0)
    lo = tp_ring(lo_part, LRP, lo_pairs, LR, LRY, ls, lr)
    lo.first(1)
    lo.first(0)

    halo2.wait_recv()
    GWT[NT] = jnp.where(ends, 0.0, HT[1].astype(F32)).astype(BF16)

    def convolve_back(g, _):
        rows = pl.ds(pl.multiple_of(g * GROUP, GROUP), GROUP)
        got = dot(windows(GWT, rows), band_of(hfwd_ref, g), ((1,), (1,)))
        for n in range(NT):
            TT[n, rows, :] = got[n * GROUP : (n + 1) * GROUP]
        return 0

    lax.fori_loop(0, GROUP, convolve_back, 0)

    def to_mixed(n, _):
        rows = tile_rows(n)
        gf, q = GF[rows, :], QKV[0, rows, :]
        gw = (gf * q).astype(BF16).astype(F32)
        gg = TT[n].T + skip_ref[...] * gw
        PF[0, rows, :] = (gf * WAVE[rows, :]).astype(BF16).astype(F32)
        PF[1, rows, :] = (gg * QKV[2, rows, :]).astype(BF16).astype(F32)
        PF[2, rows, :] = (gg * QKV[1, rows, :]).astype(BF16).astype(F32)
        return 0

    lax.fori_loop(0, NT, to_mixed, 0)
    for s in range(3):
        HS[1, s] = PF[s, 0:16, :].astype(BF16)
    halo3 = remote(HS.at[1], HR.at[1], hs.at[3], hr.at[3], prv)
    halo3.start()

    def correlate(g, _):
        rows = pl.ds(pl.multiple_of(g * GROUP, GROUP), GROUP)
        now = jnp.concatenate([GWT[n, rows, :] for n in range(NT)], axis=0)
        across = lax.broadcasted_iota(jnp.int32, (LTAPS, LTAPS), 0) + lax.broadcasted_iota(jnp.int32, (LTAPS, LTAPS), 1)
        mirror = jnp.where(across == LTAPS - 1, 1.0, 0.0).astype(BF16)
        tiles = [dot(GT[n, rows, :], mirror).astype(BF16) for n in range(NT + 1)]
        seen = jnp.concatenate(
            [jnp.concatenate([tiles[n + 1], tiles[n]], axis=1) for n in range(NT)], axis=0
        )
        pairs = dot(now, seen, ((0,), (0,)))
        TG[g] = jnp.sum(pltpu.roll(pairs, LTAPS + 1, 1, stride=1, stride_axis=0)[:, :LTAPS], axis=0, keepdims=True)
        return 0

    go.second(1)
    halo3.wait_recv()
    for s in range(3):
        head = HR[1, s].astype(F32)[0:8]
        PF[s, T : T + 8, :] = jnp.where(ends, 0.0, head)

    def short_backward(i, _):
        s, r = i // NT, lax.rem(i, NT)
        window = PF[s, pl.ds(pl.multiple_of(r * LTAPS, 8), LTAPS + 8), :]
        total = staps_ref[s, 0:1, :] * window[:LTAPS]
        for j in range(1, STAPS):
            total = total + staps_ref[s, j : j + 1, :] * pltpu.roll(window, LTAPS + 8 - j, 0)[:LTAPS]
        GM[s, pl.ds(pl.multiple_of(r * LTAPS, LTAPS), LTAPS), :] = total.astype(BF16)
        return 0

    lax.fori_loop(0, 3 * NT, short_backward, 0)

    def gin_fill(slot, half, extra, target):
        flipped = X[slot]

        def one(s, _):
            total = dot(flipped, GM[s], ((0,), (0,)))
            for ref in extra:
                total = total + ref[s].astype(F32)
            target[s] = total.astype(target.dtype)
            return 0

        lax.fori_loop(0, 3, one, 0)

    gin = ctx_ring(gin_fill, CS, CR, CSY, CRY, cs, cr)
    gin.first(1)
    go.second(0)
    gin.first(0)
    lo.second(1)
    lo.second(0)
    for pair in lo_pairs:
        pair.wait_send()
    gi_pairs = mate_pairs(GRP, gps, gpr)
    for_mate(gi_part, gi_pairs)
    lax.fori_loop(0, GROUP, correlate, 0)
    tap_sends = []
    for i in range(7):
        tap_sends.append(remote(TG, TGR.at[i], ts.at[i], tr.at[i], {"ctx": lax.rem(ctx + i + 1, 8)}))
        tap_sends[-1].start()
    gin.second(1)
    go.third()
    lo.third()
    gin.second(0)
    lo.last([LOS.at[pl.ds(0, HALF)], LOS.at[pl.ds(HALF, HALF)]])
    lo_store = pltpu.make_async_copy(LOS, lo_out, loc.at[4])
    lo_store.start()
    lo.drain()
    gi = tp_ring(gi_part, GRP, gi_pairs, GR, GRY, gs, gr)
    gi.first(1)
    gi.first(0)
    go.last([GOS.at[:, :, pl.ds(0, C)], GOS.at[:, :, pl.ds(C, C)]])
    go_store = pltpu.make_async_copy(GOS.at[0], gout_out, loc.at[5])
    go_store.start()
    gi.second(1)
    gi.second(0)
    total = TG[...]
    for i in range(7):
        tap_sends[i].wait_recv()
        total = total + TGR[i]
    for i in range(7):
        tap_sends[i].wait_send()
    TG[...] = total
    tap_store = pltpu.make_async_copy(TG, taps_out, loc.at[6])
    tap_store.start()
    gi.third()
    gin.third()
    gi.last([GIS.at[pl.ds(0, HALF)], GIS.at[pl.ds(HALF, HALF)]])
    gi_store = pltpu.make_async_copy(GIS, gi_out, loc.at[7])
    gi_store.start()
    gin.last([PF.at[:, pl.ds(0, C)], PF.at[:, pl.ds(C, C)]])
    gin_store = pltpu.make_async_copy(PF.at[:, pl.ds(0, 2 * C)], gin_out, loc.at[8])
    gin_store.start()

    gx.drain()
    gy.drain()
    go.drain()
    gi.drain()
    gin.drain()
    for pair in gi_pairs:
        pair.wait_send()
    for copy in (halo0, halo1, halo2, halo3):
        copy.wait_send()
    for store in (lo_store, go_store, tap_store, gi_store, gin_store):
        store.wait()


def local(inputs, in_proj, out_proj, short_taps, skip_gain, long_taps, cotangent):
    d = in_proj.shape[0]
    n_tp = d // C
    w = jnp.transpose(in_proj, (1, 0, 2))
    staps = jnp.transpose(short_taps, (1, 0, 2))
    taps = long_taps.astype(F32).T
    zeros = jnp.zeros((GROUP, LTAPS), F32)
    hfwd = jnp.concatenate([taps, zeros], axis=1).reshape(GROUP, 1, 2 * LTAPS)
    hrev = jnp.concatenate([zeros[:, :1], taps[:, ::-1], zeros[:, 1:]], axis=1).reshape(GROUP, 1, 2 * LTAPS)
    vm = pltpu.VMEM
    sem = pltpu.SemaphoreType.DMA
    scratch = [
        vm((n_tp, T, C), BF16), vm((n_tp, T, C), BF16), vm((3, d, C), BF16), vm((C, d), BF16),
        vm((3, T + 8, C), F32), vm((3, T, C), F32), vm((T, C), F32), vm((T, C), F32),
        vm((T, C), BF16), vm((C, T), BF16), vm((3, T, C), BF16),
        vm((NT + 1, C, LTAPS), BF16), vm((NT + 1, C, LTAPS), BF16), vm((NT, C, LTAPS), F32),
        vm((2, 3, 16, C), BF16), vm((2, 3, 16, C), BF16), vm((2, C, LTAPS), BF16),
        vm((GROUP, 1, LTAPS), F32), vm((7, GROUP, 1, LTAPS), F32),
        vm((1, C, 2 * C), F32), vm((T, C), BF16), vm((T, C), BF16),
        vm((8, 2, HALF, C), BF16), vm((8, 2, HALF, C), BF16), vm((8, 2, HALF, C), BF16),
        vm((2, 6, HALF, C), BF16), vm((2, 6, HALF, C), BF16), vm((2, 6, HALF, C), BF16),
        vm((2, HALF, C), BF16), vm((2, HALF, C), BF16), vm((2, HALF, C), BF16),
        vm((2, 6, 3, C, C), BF16), vm((2, 6, 3, C, C), BF16), vm((2, 3, C, C), BF16), vm((2, 3, C, C), BF16),
        vm((2, 6, 1, C, C), BF16), vm((2, 6, 1, C, C), BF16), vm((2, 1, C, C), BF16), vm((2, 1, C, C), BF16),
        sem((17,)), sem((17,)), sem((17,)), sem((17,)),
        sem((8,)), sem((8,)), sem((8,)), sem((8,)),
        sem((9,)), sem((9,)), sem((9,)), sem((9,)),
        sem((9,)), sem((9,)), sem((9,)), sem((9,)),
        sem((4,)), sem((4,)), sem((7,)), sem((7,)), sem((9,)),
    ]
    hbm = pl.BlockSpec(memory_space=pl.ANY)
    vmem = pl.BlockSpec(memory_space=pltpu.VMEM)
    layer_out, grad_inputs, grad_in, grad_out, tap_rows = pl.pallas_call(
        body,
        out_shape=[
            jax.ShapeDtypeStruct((T, C), BF16),
            jax.ShapeDtypeStruct((T, C), BF16),
            jax.ShapeDtypeStruct((3, 2 * C, C), F32),
            jax.ShapeDtypeStruct((C, 2 * C), F32),
            jax.ShapeDtypeStruct((GROUP, 1, LTAPS), F32),
        ],
        in_specs=[hbm, hbm, hbm, hbm, vmem, vmem, vmem, vmem],
        out_specs=[hbm] * 5,
        scratch_shapes=scratch,
        compiler_params=pltpu.CompilerParams(
            collective_id=0, has_side_effects=True, vmem_limit_bytes=67043328
        ),
    )(inputs, cotangent, w, out_proj, staps, skip_gain.reshape(1, C), hrev, hfwd)
    grad_taps = tap_rows.reshape(GROUP, LTAPS).T
    return (layer_out, grad_inputs, jnp.transpose(grad_in, (1, 0, 2)), grad_out, grad_taps)


def solution(mesh):
    placed = (
        P("ctx", "tp"),
        P(None, None, "tp"),
        P("tp", None),
        P(None, None, "tp"),
        P("tp"),
        P(None, "tp"),
        P("ctx", "tp"),
    )
    return jax.shard_map(
        local,
        mesh=mesh,
        in_specs=placed,
        out_specs=(
            P("ctx", "tp"),
            P("ctx", "tp"),
            P("ctx", None, "tp"),
            P("tp", "ctx"),
            P(None, "tp"),
        ),
        check_vma=False,
    )
```

time: 507 us -> 179 us (0.35)
  waiting for transfers between devices: 309 us -> 0 us
  Pallas kernels: 0 us -> 169 us
  local copies, waits for them, and re-layouts: 72.2 us -> 7.66 us
  matrix products: 59.6 us -> 0 us
  blocking collectives: 22.4 us -> 0 us
  other arithmetic: 16.4 us -> 0.77 us
  between operations: 14.6 us -> 0.66 us
  starting transfers between devices: 11.1 us -> 0 us
    reduce_scatter x4 -> x0, waiting for transfers between devices: 199 us -> none  [the longest x1 93.7 us: local(): lax.psum_scatter(input_terms.astype(jnp.bfloat16), 'tp', scatter_dimensio...]
    pallas_call x0 -> x1, Pallas kernels: none -> 169 us  [local(): pl.pallas_call(body, out_shape=[jax.ShapeDtypeStruct((T, C), BF16), jax.S...]
    all_gather x2 -> x0, waiting for transfers between devices: 104 us -> none  [the longest x1 60.1 us: local(): inputs_full = lax.all_gather(inputs, 'tp', axis=1, tiled=True)]
    dot_general x14 -> x0, matrix products: 59.6 us -> none  [the longest x1 9.73 us: local(): lax.dot_general(grad_matrix, in_matrix, (((1,), (1,)), ((), ())), preferr...]
    psum x1 -> x0, blocking collectives: 22.4 us -> none  [local(): grad_long_taps = lax.psum(tap_grads.T, 'ctx')]
    reshape x5 -> x2, local copies, waits for them, and re-layouts: 16.5 us -> 1.25 us  [the longest x1 0.63 us: local(): jnp.concatenate([zeros[:, :1], taps[:, ::-1], zeros[:, 1:]], axis=1)]
    rev x2 -> x1, local copies, waits for them, and re-layouts: 15 us -> 0.07 us  [local(): taps[:, ::-1]]
    unnamed x56 -> x11, local copies, waits for them, and re-layouts: 19.3 us -> 6.25 us
  transfers between devices with their start and end apart: 10 -> 0, of which waited for: 6 -> 0; matrix products, arithmetic and copies ran while one was open for 21% -> 0% of each run, Pallas kernels for 0% -> 0%
where the time goes in v1:
time: 179 us; the launch traced here: 178 us
  Pallas kernels  169 us (94%)
  local copies, waits for them, and re-layouts  7.66 us (4%)
    pallas_call x1, Pallas kernels, local(): pl.pallas_call(body, out_shape=[jax.ShapeDtypeStruct((T, C), BF16), jax.S...  169 us
    unnamed x11, local copies, waits for them, and re-layouts  6.25 us

profile of v1, /device:TPU:0, one launch (start us, length us, event | category | flops | bytes accessed | tf_op | source)
XLA Modules:
  0.0 178.3 jit_solution(12651128616860689625)
XLA Ops:
  0.6 0.1 pad.3.clone
  0.7 0.7 convert_bitcast_fusion
  1.4 0.1 rev.3
  1.5 0.1 maximum_bitcast_fusion
  1.6 0.6 copy.12.hrev_ref
  2.2 0.6 reshape.24.hfwd_ref
  2.8 169.2 %shard_map.110 = (bf16[768,256]{1,0:T(8,128)(2,1)}, bf16[768,256]{1,0:T(8,128)(2,1)}, f32[3,512,256]{2,1,0:T(8,128)}, f32[256,512]{1,0:T(8,128)}, f32[16,1,128]{2,1,0:T(1,128)}) custom-call(bf16[768,256]{1,0:T(8,128)(2,1)} %inputs_ref.1, bf16[768,256]{1,0:T(8,128)(2,1)} %cot_ref.1, bf16[3,4096,256]{2,1,0:T(8,128)(2,1)} %bitcast.12, ...), custom_call_target="tpu_custom_call" | custom-call | tf_op jit(solution)/shard_map/pallas_call | solution.py:582
  172.0 0.0 copy-start
  172.0 1.9 %copy.18 = bf16[768,256]{1,0:T(8,128)(2,1)} copy(bf16[768,256]{1,0:T(8,128)(2,1)} %get-tuple-element.20) | data formatting | bytes 786432
  173.9 0.0 copy-start.1
  173.9 1.8 %copy.19 = bf16[768,256]{1,0:T(8,128)(2,1)} copy(bf16[768,256]{1,0:T(8,128)(2,1)} %get-tuple-element.21) | data formatting | bytes 786432
  175.8 0.0 copy-done
  175.8 0.0 copy-start.2
  175.8 1.1 copy.20
  176.9 0.0 copy-done.1
  176.9 0.8 copy.21
  177.7 0.0 copy-done.2
  177.7 0.6 copy.22
  (3 shorter events, 0.0 us)
Async XLA Ops:
  172.0 3.7 %copy-start = (f32[3,512,256]{2,1,0:T(8,128)S(1)}, f32[3,512,256]{2,1,0:T(8,128)}, u32[]{:S(2)}) copy-start(f32[3,512,256]{2,1,0:T(8,128)} %get-tuple-element.12) | copy-start | bytes 4718596
  173.9 3.0 %copy-start.1 = (f32[256,512]{1,0:T(8,128)S(1)}, f32[256,512]{1,0:T(8,128)}, u32[]{:S(2)}) copy-start(f32[256,512]{1,0:T(8,128)} %get-tuple-element.23) | copy-start | bytes 1572868
  175.8 1.9 %copy-start.2 = (f32[16,1,128]{2,1,0:T(1,128)S(1)}, f32[16,1,128]{2,1,0:T(1,128)}, u32[]{:S(2)}) copy-start(f32[16,1,128]{2,1,0:T(1,128)} %get-tuple-element.14) | copy-start | bytes 24580

commit v2 on v1

--- a/solution.py
+++ b/solution.py
@@ -133,6 +133,10 @@
         for half in range(2):
             self.part("c", 0, half, [r.at[0, 2 + half], r.at[0, 4 + half], self.side_in.at[half]], targets[half])
 
+    def sent(self, *which):
+        for i in which:
+            self.copies[i].wait_send()
+
     def drain(self):
         for copy in self.copies:
             copy.wait_send()
@@ -167,6 +171,7 @@
     gx = Gather(inputs_ref, X, xs, xr, z, h, k)
     gy = Gather(cot_ref, Y, ys, yr, z, h, k)
     gx.start(2, 0, 1, 3)
+    gy.start(2)
     loads = [
         pltpu.make_async_copy(inputs_ref, X.at[me], loc.at[0]),
         pltpu.make_async_copy(w_hbm, W, loc.at[1]),
@@ -198,24 +203,27 @@
     gx.start(7, 9)
     gx.wait(1)
     gx.start(8, 10)
+    gy.start(0, 1, 3)
     project(1)
+    gx.wait(9, 10)
+    project(2)
+    gx.wait(7, 8)
+    gx.start(15)
     gx.wait(2)
     gx.start(4, 5, 6)
-    gy.start(2)
-    gx.wait(9, 10)
-    project(2)
+    gx.wait(15)
+    project(6)
     gx.wait(6)
     project(3)
-    gx.wait(7, 8)
-    gx.start(15)
     gx.wait(4)
     gx.start(11, 13)
     gx.wait(5)
     gx.start(12, 14)
-    gy.start(0, 1, 3)
+    gy.wait(0, 1)
+    gy.start(7, 9, 8, 10)
     project(4)
-    gx.wait(15)
-    project(6)
+    gy.wait(2)
+    gy.start(4, 5, 6)
     gx.wait(13, 14)
     project(5)
     gx.wait(11, 12)
@@ -235,12 +243,6 @@
     halo0 = remote(HS.at[0], HR.at[0], hs.at[0], hr.at[0], nxt)
     halo0.start()
     lax.fori_loop(0, 3 * NT, round_rows, 0)
-    gy.wait(2)
-    gy.start(4, 5, 6)
-    gy.wait(0)
-    gy.start(7, 9)
-    gy.wait(1)
-    gy.start(8, 10)
     halo0.wait_recv()
     begins, ends = ctx == 0, ctx == 7
     for s in range(3):
@@ -271,10 +273,6 @@
     lax.fori_loop(0, NT, put_gated, 0)
     halo1 = remote(GT.at[NT], HT.at[0], hs.at[1], hr.at[1], nxt)
     halo1.start()
-    gy.wait(4)
-    gy.start(11, 13)
-    gy.wait(5)
-    gy.start(12, 14)
     gy.wait(7, 8)
     gy.start(15)
     halo1.wait_recv()
@@ -297,6 +295,10 @@
         return 0
 
     lax.fori_loop(0, GROUP, convolve, 0)
+    gy.wait(4)
+    gy.start(11, 13)
+    gy.wait(5)
+    gy.start(12, 14)
 
     for n in range(NT):
         rows = pl.ds(n * LTAPS, LTAPS)
@@ -383,13 +385,16 @@
     filter_grad(2)
     gy.wait(6)
     filter_grad(3)
-    gy.wait(11, 12)
-    gy.start(16)
     filter_grad(4)
     gy.wait(15)
     filter_grad(6)
     gy.wait(13, 14)
     filter_grad(5)
+    lo = tp_ring(lo_part, LRP, lo_pairs, LR, LRY, ls, lr)
+    lo.first(1)
+    lo.first(0)
+    gy.wait(11, 12)
+    gy.start(16)
     gy.wait(16)
     filter_grad(7)
 
@@ -411,9 +416,6 @@
     go = ctx_ring(go_fill, OS, OR, OSY, ORY, os_, or_)
     go.first(1)
     go.first(0)
-    lo = tp_ring(lo_part, LRP, lo_pairs, LR, LRY, ls, lr)
-    lo.first(1)
-    lo.first(0)
 
     halo2.wait_recv()
     GWT[NT] = jnp.where(ends, 0.0, HT[1].astype(F32)).astype(BF16)
@@ -442,6 +444,8 @@
         HS[1, s] = PF[s, 0:16, :].astype(BF16)
     halo3 = remote(HS.at[1], HR.at[1], hs.at[3], hr.at[3], prv)
     halo3.start()
+    lo.second(1)
+    lo.second(0)
 
     def correlate(g, _):
         rows = pl.ds(pl.multiple_of(g * GROUP, GROUP), GROUP)
@@ -487,35 +491,39 @@
 
     gin = ctx_ring(gin_fill, CS, CR, CSY, CRY, cs, cr)
     gin.first(1)
+    gin.first(0)
     go.second(0)
-    gin.first(0)
-    lo.second(1)
-    lo.second(0)
     for pair in lo_pairs:
         pair.wait_send()
     gi_pairs = mate_pairs(GRP, gps, gpr)
     for_mate(gi_part, gi_pairs)
+    lo.third()
+    go.third()
+    gi = tp_ring(gi_part, GRP, gi_pairs, GR, GRY, gs, gr)
+    lo.sent(4, 5)
+    gi.first(1)
+    lo.sent(0, 1)
+    gi.first(0)
+    gin.second(1)
+    lo.sent(6, 7)
+    gi.second(1)
+    gin.second(0)
+    lo.sent(2, 3)
+    gi.second(0)
     lax.fori_loop(0, GROUP, correlate, 0)
     tap_sends = []
     for i in range(7):
         tap_sends.append(remote(TG, TGR.at[i], ts.at[i], tr.at[i], {"ctx": lax.rem(ctx + i + 1, 8)}))
         tap_sends[-1].start()
-    gin.second(1)
-    go.third()
-    lo.third()
-    gin.second(0)
+    lo.sent(8)
+    gi.third()
     lo.last([LOS.at[pl.ds(0, HALF)], LOS.at[pl.ds(HALF, HALF)]])
     lo_store = pltpu.make_async_copy(LOS, lo_out, loc.at[4])
     lo_store.start()
-    lo.drain()
-    gi = tp_ring(gi_part, GRP, gi_pairs, GR, GRY, gs, gr)
-    gi.first(1)
-    gi.first(0)
     go.last([GOS.at[:, :, pl.ds(0, C)], GOS.at[:, :, pl.ds(C, C)]])
     go_store = pltpu.make_async_copy(GOS.at[0], gout_out, loc.at[5])
     go_store.start()
-    gi.second(1)
-    gi.second(0)
+    gin.third()
     total = TG[...]
     for i in range(7):
         tap_sends[i].wait_recv()
@@ -525,8 +533,6 @@
     TG[...] = total
     tap_store = pltpu.make_async_copy(TG, taps_out, loc.at[6])
     tap_store.start()
-    gi.third()
-    gin.third()
     gi.last([GIS.at[pl.ds(0, HALF)], GIS.at[pl.ds(HALF, HALF)]])
     gi_store = pltpu.make_async_copy(GIS, gi_out, loc.at[7])
     gi_store.start()

time: 179 us -> 166 us (0.927)
  Pallas kernels: 169 us -> 157 us
    pallas_call x1, Pallas kernels: 169 us -> 157 us  [local(): pl.pallas_call(body, out_shape=[jax.ShapeDtypeStruct((T, C), BF16), jax.S...]
where the time goes in v2:
time: 166 us
  Pallas kernels  157 us (95%)
  local copies, waits for them, and re-layouts  7.66 us (5%)
    pallas_call x1, Pallas kernels, local(): pl.pallas_call(body, out_shape=[jax.ShapeDtypeStruct((T, C), BF16), jax.S...  157 us
    unnamed x11, local copies, waits for them, and re-layouts  6.25 us

profile of v2, /device:TPU:0, one launch (start us, length us, event | category | flops | bytes accessed | tf_op | source)
XLA Modules:
  0.0 165.7 jit_solution(941725835212765461)
XLA Ops:
  0.6 0.1 pad.3.clone
  0.7 0.7 convert_bitcast_fusion
  1.4 0.1 rev.3
  1.5 0.1 maximum_bitcast_fusion
  1.6 0.6 copy.12.hrev_ref
  2.2 0.6 reshape.24.hfwd_ref
  2.8 156.6 %shard_map.110 = (bf16[768,256]{1,0:T(8,128)(2,1)}, bf16[768,256]{1,0:T(8,128)(2,1)}, f32[3,512,256]{2,1,0:T(8,128)}, f32[256,512]{1,0:T(8,128)}, f32[16,1,128]{2,1,0:T(1,128)}) custom-call(bf16[768,256]{1,0:T(8,128)(2,1)} %inputs_ref.1, bf16[768,256]{1,0:T(8,128)(2,1)} %cot_ref.1, bf16[3,4096,256]{2,1,0:T(8,128)(2,1)} %bitcast.12, ...), custom_call_target="tpu_custom_call" | custom-call | tf_op jit(solution)/shard_map/pallas_call | solution.py:588
  159.5 0.0 copy-start
  159.5 1.9 %copy.18 = bf16[768,256]{1,0:T(8,128)(2,1)} copy(bf16[768,256]{1,0:T(8,128)(2,1)} %get-tuple-element.20) | data formatting | bytes 786432
  161.4 0.0 copy-start.1
  161.4 1.8 %copy.19 = bf16[768,256]{1,0:T(8,128)(2,1)} copy(bf16[768,256]{1,0:T(8,128)(2,1)} %get-tuple-element.21) | data formatting | bytes 786432
  163.2 0.0 copy-done
  163.2 0.0 copy-start.2
  163.2 1.1 copy.20
  164.3 0.0 copy-done.1
  164.3 0.8 copy.21
  165.1 0.0 copy-done.2
  165.1 0.6 copy.22
  (3 shorter events, 0.0 us)
Async XLA Ops:
  159.5 3.7 %copy-start = (f32[3,512,256]{2,1,0:T(8,128)S(1)}, f32[3,512,256]{2,1,0:T(8,128)}, u32[]{:S(2)}) copy-start(f32[3,512,256]{2,1,0:T(8,128)} %get-tuple-element.12) | copy-start | bytes 4718596
  161.4 3.0 %copy-start.1 = (f32[256,512]{1,0:T(8,128)S(1)}, f32[256,512]{1,0:T(8,128)}, u32[]{:S(2)}) copy-start(f32[256,512]{1,0:T(8,128)} %get-tuple-element.23) | copy-start | bytes 1572868
  163.2 1.9 %copy-start.2 = (f32[16,1,128]{2,1,0:T(1,128)S(1)}, f32[16,1,128]{2,1,0:T(1,128)}, u32[]{:S(2)}) copy-start(f32[16,1,128]{2,1,0:T(1,128)} %get-tuple-element.14) | copy-start | bytes 24580

commit v3 on v2

--- a/solution.py
+++ b/solution.py
@@ -93,13 +93,14 @@
         self.out, self.inn, self.side_out, self.side_in = out, inn, side_out, side_in
         self.part = part
         self.copies = []
-        for kind in range(2):
+        for kind in range(out.shape[0]):
             for i, (low, size, where) in enumerate([(0, 1, plus), (1, 1, minus), (2, 2, plus), (4, 2, minus)]):
                 span = pl.ds(low, size)
                 self.copies.append(
                     remote(out.at[kind, span], inn.at[kind, span], send.at[kind * 4 + i], recv.at[kind * 4 + i], where)
                 )
-        self.copies.append(remote(side_out, side_in, send.at[8], recv.at[8], side))
+        if side is not None:
+            self.copies.append(remote(side_out, side_in, send.at[8], recv.at[8], side))
 
     def first(self, kind):
         for half in range(2):
@@ -129,9 +130,11 @@
         r = self.inn
         self.copies[2].wait_recv()
         self.copies[3].wait_recv()
-        self.copies[8].wait_recv()
+        if self.side_in is not None:
+            self.copies[8].wait_recv()
         for half in range(2):
-            self.part("c", 0, half, [r.at[0, 2 + half], r.at[0, 4 + half], self.side_in.at[half]], targets[half])
+            extra = [] if self.side_in is None else [self.side_in.at[half]]
+            self.part("c", 0, half, [r.at[0, 2 + half], r.at[0, 4 + half]] + extra, targets[half])
 
     def sent(self, *which):
         for i in which:
@@ -146,8 +149,9 @@
     inputs_ref, cot_ref, w_hbm, op_hbm, staps_ref, skip_ref, hrev_ref, hfwd_ref,
     lo_out, gi_out, gin_out, gout_out, taps_out,
     X, Y, W, OP, PF, QKV, WAVE, GF, FIL, FT, GM, GT, GWT, TT, HS, HR, HT, TG, TGR, GOS, LOS, GIS,
+    YS, YR, BS, BR,
     SP, LRP, GRP, S, LR, GR, SY, LRY, GRY, CS, CR, CSY, CRY, OS, OR, OSY, ORY,
-    xs, xr, ys, yr, lps, lpr, gps, gpr, ls, lr, gs, gr, cs, cr, os_, or_, hs, hr, ts, tr, loc,
+    xs, xr, ys, yr, lps, lpr, gps, gpr, ls, lr, gs, gr, cs, cr, os_, or_, hs, hr, ts, tr, loc, fs, fr, bs, br,
 ):
     ctx = lax.axis_index("ctx")
     me = lax.axis_index("tp")
@@ -487,10 +491,33 @@
             target[s] = total.astype(target.dtype)
             return 0
 
-        lax.fori_loop(0, 3, one, 0)
+        lax.fori_loop(0, 2, one, 0)
 
     gin = ctx_ring(gin_fill, CS, CR, CSY, CRY, cs, cr)
+    flat_pairs = [remote(YS.at[i], YR.at[i], fs.at[i], fr.at[i], {"ctx": (1 - l) * 4 + x}) for i in range(4)]
+    places = (xo, xp, xm, x)
+
+    def flat_part(ll, i, half):
+        return dot(X[(ll * 4 + places[i]) * 2 + half], GM[2], ((0,), (0,)))
+
+    def flat_term(name, kind, half, extra, target):
+        i = {"o": 0, "p": 1, "m": 2, "c": 3}[name]
+        if half == 0:
+            flat_pairs[i].wait_recv()
+        total = flat_part(l, i, half) + YR[i, half].astype(F32)
+        for ref in extra:
+            total = total + ref[...].astype(F32)
+        target[...] = total.astype(target.dtype)
+
+    flat = Ring(BS, BR, None, None, bs, br, {"ctx": l * 4 + xp}, {"ctx": l * 4 + xm}, None, flat_term)
     gin.first(1)
+    for i in range(4):
+        def one(half, _, i=i):
+            YS[i, half] = flat_part(1 - l, i, half).astype(BF16)
+            return 0
+
+        lax.fori_loop(0, 2, one, 0)
+        flat_pairs[i].start()
     gin.first(0)
     go.second(0)
     for pair in lo_pairs:
@@ -504,9 +531,11 @@
     gi.first(1)
     lo.sent(0, 1)
     gi.first(0)
+    flat.first(0)
     gin.second(1)
     lo.sent(6, 7)
     gi.second(1)
+    flat.second(0)
     gin.second(0)
     lo.sent(2, 3)
     gi.second(0)
@@ -536,6 +565,7 @@
     gi.last([GIS.at[pl.ds(0, HALF)], GIS.at[pl.ds(HALF, HALF)]])
     gi_store = pltpu.make_async_copy(GIS, gi_out, loc.at[7])
     gi_store.start()
+    flat.last([PF.at[2, pl.ds(0, C)], PF.at[2, pl.ds(C, C)]])
     gin.last([PF.at[:, pl.ds(0, C)], PF.at[:, pl.ds(C, C)]])
     gin_store = pltpu.make_async_copy(PF.at[:, pl.ds(0, 2 * C)], gin_out, loc.at[8])
     gin_store.start()
@@ -545,6 +575,9 @@
     go.drain()
     gi.drain()
     gin.drain()
+    flat.drain()
+    for pair in flat_pairs:
+        pair.wait_send()
     for pair in gi_pairs:
         pair.wait_send()
     for copy in (halo0, halo1, halo2, halo3):
@@ -572,16 +605,18 @@
         vm((2, 3, 16, C), BF16), vm((2, 3, 16, C), BF16), vm((2, C, LTAPS), BF16),
         vm((GROUP, 1, LTAPS), F32), vm((7, GROUP, 1, LTAPS), F32),
         vm((1, C, 2 * C), F32), vm((T, C), BF16), vm((T, C), BF16),
+        vm((4, 2, C, C), BF16), vm((4, 2, C, C), BF16), vm((1, 6, C, C), BF16), vm((1, 6, C, C), BF16),
         vm((8, 2, HALF, C), BF16), vm((8, 2, HALF, C), BF16), vm((8, 2, HALF, C), BF16),
         vm((2, 6, HALF, C), BF16), vm((2, 6, HALF, C), BF16), vm((2, 6, HALF, C), BF16),
         vm((2, HALF, C), BF16), vm((2, HALF, C), BF16), vm((2, HALF, C), BF16),
-        vm((2, 6, 3, C, C), BF16), vm((2, 6, 3, C, C), BF16), vm((2, 3, C, C), BF16), vm((2, 3, C, C), BF16),
+        vm((2, 6, 2, C, C), BF16), vm((2, 6, 2, C, C), BF16), vm((2, 2, C, C), BF16), vm((2, 2, C, C), BF16),
         vm((2, 6, 1, C, C), BF16), vm((2, 6, 1, C, C), BF16), vm((2, 1, C, C), BF16), vm((2, 1, C, C), BF16),
         sem((17,)), sem((17,)), sem((17,)), sem((17,)),
         sem((8,)), sem((8,)), sem((8,)), sem((8,)),
         sem((9,)), sem((9,)), sem((9,)), sem((9,)),
         sem((9,)), sem((9,)), sem((9,)), sem((9,)),
         sem((4,)), sem((4,)), sem((7,)), sem((7,)), sem((9,)),
+        sem((4,)), sem((4,)), sem((4,)), sem((4,)),
     ]
     hbm = pl.BlockSpec(memory_space=pl.ANY)
     vmem = pl.BlockSpec(memory_space=pltpu.VMEM)

time: 166 us -> 161 us (0.970)
  Pallas kernels: 157 us -> 152 us
    pallas_call x1, Pallas kernels: 157 us -> 152 us  [local(): pl.pallas_call(body, out_shape=[jax.ShapeDtypeStruct((T, C), BF16), jax.S...]
where the time goes in v3:
time: 161 us
  Pallas kernels  152 us (94%)
  local copies, waits for them, and re-layouts  7.66 us (5%)
    pallas_call x1, Pallas kernels, local(): pl.pallas_call(body, out_shape=[jax.ShapeDtypeStruct((T, C), BF16), jax.S...  152 us
    unnamed x11, local copies, waits for them, and re-layouts  6.25 us

profile of v3, /device:TPU:0, one launch (start us, length us, event | category | flops | bytes accessed | tf_op | source)
XLA Modules:
  0.0 160.8 jit_solution(4362003693522703050)
XLA Ops:
  0.6 0.1 pad.3.clone
  0.7 0.7 convert_bitcast_fusion
  1.4 0.1 rev.3
  1.5 0.1 maximum_bitcast_fusion
  1.6 0.6 copy.12.hrev_ref
  2.2 0.6 reshape.24.hfwd_ref
  2.8 151.7 %shard_map.110 = (bf16[768,256]{1,0:T(8,128)(2,1)}, bf16[768,256]{1,0:T(8,128)(2,1)}, f32[3,512,256]{2,1,0:T(8,128)}, f32[256,512]{1,0:T(8,128)}, f32[16,1,128]{2,1,0:T(1,128)}) custom-call(bf16[768,256]{1,0:T(8,128)(2,1)} %inputs_ref.1, bf16[768,256]{1,0:T(8,128)(2,1)} %cot_ref.1, bf16[3,4096,256]{2,1,0:T(8,128)(2,1)} %bitcast.12, ...), custom_call_target="tpu_custom_call" | custom-call | tf_op jit(solution)/shard_map/pallas_call | solution.py:623
  154.5 0.0 copy-start
  154.5 1.9 %copy.18 = bf16[768,256]{1,0:T(8,128)(2,1)} copy(bf16[768,256]{1,0:T(8,128)(2,1)} %get-tuple-element.20) | data formatting | bytes 786432
  156.4 0.0 copy-start.1
  156.4 1.8 %copy.19 = bf16[768,256]{1,0:T(8,128)(2,1)} copy(bf16[768,256]{1,0:T(8,128)(2,1)} %get-tuple-element.21) | data formatting | bytes 786432
  158.2 0.0 copy-done
  158.3 0.0 copy-start.2
  158.3 1.1 copy.20
  159.4 0.0 copy-done.1
  159.4 0.8 copy.21
  160.2 0.0 copy-done.2
  160.2 0.6 copy.22
  (3 shorter events, 0.0 us)
Async XLA Ops:
  154.5 3.7 %copy-start = (f32[3,512,256]{2,1,0:T(8,128)S(1)}, f32[3,512,256]{2,1,0:T(8,128)}, u32[]{:S(2)}) copy-start(f32[3,512,256]{2,1,0:T(8,128)} %get-tuple-element.12) | copy-start | bytes 4718596
  156.4 3.0 %copy-start.1 = (f32[256,512]{1,0:T(8,128)S(1)}, f32[256,512]{1,0:T(8,128)}, u32[]{:S(2)}) copy-start(f32[256,512]{1,0:T(8,128)} %get-tuple-element.23) | copy-start | bytes 1572868
  158.3 1.9 %copy-start.2 = (f32[16,1,128]{2,1,0:T(1,128)S(1)}, f32[16,1,128]{2,1,0:T(1,128)}, u32[]{:S(2)}) copy-start(f32[16,1,128]{2,1,0:T(1,128)} %get-tuple-element.14) | copy-start | bytes 24580
